TPU v7x, 128 devices: a whole 4x4x4 slice. The times are simulated.
128 devices in a mesh: blk: 16 (over x, z), beam: 8 (over y, core).
Axes of the slice: x: 4, y: 4, z: 4, core: 2. Of those that a mesh axis runs over, the one named last changes fastest.
Arguments:
- embeds: bfloat16 [4, 128, 2048], P(None, 'beam'), may hold values from -6 to 6
- attn_gain: float32 [2048], replicated, may hold values from 0.25 to 1.75
- w_query: bfloat16 [2048, 3072], P(None, 'blk'), may hold values from -0.125 to 0.125
- w_latent: bfloat16 [2048, 576], replicated, may hold values from -0.125 to 0.125
- latent_gain: float32 [512], replicated, may hold values from 0.3 to 3
- w_key_up: bfloat16 [16, 128, 512], P('blk'), may hold values from -0.5 to 0.5
- w_value_up: bfloat16 [16, 512, 128], P('blk'), may hold values from -0.25 to 0.25
- w_out: bfloat16 [2048, 2048], P('blk'), may hold values from -0.125 to 0.125
- ffn_gain: float32 [2048], replicated, may hold values from 0.25 to 1.75
- w_shared_gate: bfloat16 [2048, 2816], P(None, 'blk'), may hold values from -0.125 to 0.125
- w_shared_up: bfloat16 [2048, 2816], P(None, 'blk'), may hold values from -0.125 to 0.125
- w_shared_down: bfloat16 [2816, 2048], P('blk'), may hold values from -0.109375 to 0.109375
- w_expert_gate: bfloat16 [32, 2048, 2816], P('blk', None, 'beam'), may hold values from -0.125 to 0.125
- w_expert_up: bfloat16 [32, 2048, 2816], P('blk', None, 'beam'), may hold values from -0.125 to 0.125
- w_expert_down: bfloat16 [32, 2816, 2048], P('blk', 'beam'), may hold values from -0.15625 to 0.15625
- cache_pool: bfloat16 [16, 96, 128, 576], P('beam', 'blk'), may hold values from -1600 to 1600
- block_tables: int32 [16, 8, 64], P('beam'), may hold values from 0 to 95, as said below
- block_counts: int32 [16], P('beam'), may hold values from 4 to 64
- parents: int32 [4, 16, 8], P(None, 'beam'), may hold values from 0 to 7
- expert_ids: int32 [4, 128, 6], replicated, may hold values from 0 to 63, all different within a row; in each aligned block of 128 rows (0 to 127, 128 to 255, ..., all dimensions but the last counted through in order) at most 24 rows name the same one
- expert_weights: float32 [4, 128, 6], replicated, may hold values from 0.1 to 0.6
Outputs:
- layer_out: float32 [4, 128, 2048], P(None, ('blk', 'beam'))
Inputs may be any that keep to these rules, and one draw needn't show every extreme that they name: `block_tables`: for each group g, entries j below block_counts[g] of one beam name different physical blocks; entries at or beyond block_counts[g] are never read. `expert_ids`: the experts of one row differ; within one step all rows together name one expert at most 24 times.
All inputs are finite; a program needn't handle non-finite values.
Results may differ from a plain program's by a relative error of at most 0.034.
Values may be sent and summed in bfloat16 or wider, within the bound.
No kernel may reach another device: no remote copies, remote signals or barrier semaphores. Data moves between devices by JAX's collectives and lax.ppermute only.
A program may use at most 128 MiB of HBM per device.

v0:
```python
import jax
import jax.numpy as jnp
from jax import lax
from jax.sharding import PartitionSpec as P

EXPERTS = 64
FFE = 1408
THETA = 50000.0
EPS = 1e-06
NEG = -1e30


def combined_all(shard, axis, combine):
    everything = jax.tree.map(lambda part: lax.all_gather(part, axis), shard)
    initial = jax.tree.map(lambda part: part[0], everything)

    def step(k, so_far):
        return combine(so_far, jax.tree.map(lambda part: part[k], everything))

    return lax.fori_loop(1, lax.axis_size(axis), step, initial)


def rms_scale(values, gain):
    mean_sq = jnp.mean(values * values, axis=-1, keepdims=True)
    return values * lax.rsqrt(mean_sq + EPS) * gain


def rotate(values, position):
    half_dim = values.shape[-1] // 2
    frequency = THETA ** (-jnp.arange(half_dim, dtype=jnp.float32) * 2.0 / values.shape[-1])
    angles = position[..., None] * frequency
    cosine = jnp.cos(angles)
    sine_part = jnp.sin(angles)
    lower_half = values[..., :half_dim]
    upper_half = values[..., half_dim:]
    return jnp.concatenate(
        [
            lower_half * cosine - upper_half * sine_part,
            lower_half * sine_part + upper_half * cosine,
        ],
        axis=-1,
    )


def combine(earlier, later):
    top_first, sum_first, lat_first = earlier
    top_second, sum_second, lat_second = later
    top_score = jnp.maximum(top_first, top_second)
    scale_first = jnp.exp(top_first - top_score)
    scale_second = jnp.exp(top_second - top_score)
    return (
        top_score,
        sum_first * scale_first + sum_second * scale_second,
        lat_first * scale_first[..., None] + lat_second * scale_second[..., None],
    )


def partial_attend(scores, key_mask, values, form):
    masked = jnp.where(key_mask, scores, NEG)
    top_score = jnp.max(masked, axis=-1)
    weights = jnp.where(key_mask, jnp.exp(masked - top_score[..., None]), 0.0)
    weight_sum = jnp.sum(weights, axis=-1)
    latent_sum = jnp.einsum(
        form, weights.astype(jnp.bfloat16), values, preferred_element_type=jnp.float32
    )
    return (top_score, weight_sum, latent_sum)


def per_device(
    embeds,
    attn_gain,
    w_query,
    w_latent,
    latent_gain,
    w_key_up,
    w_value_up,
    w_out,
    ffn_gain,
    w_shared_gate,
    w_shared_up,
    w_shared_down,
    w_expert_gate,
    w_expert_up,
    w_expert_down,
    cache_pool,
    block_tables,
    block_counts,
    parents,
    expert_ids,
    expert_weights,
):
    step_count, row_dev, model_width = embeds.shape
    group_count, beam_count, max_blocks = block_tables.shape
    heads_dev, head_in, latent = w_key_up.shape
    entry_width = cache_pool.shape[3]
    pool_dev = cache_pool.shape[1]
    block_len = cache_pool.shape[2]
    value_dim = w_value_up.shape[2]
    pair_dev = w_expert_gate.shape[0]
    unit_dev = w_expert_gate.shape[2]
    topk_count = expert_ids.shape[2]
    blk_index = lax.axis_index("blk")
    beam_index = lax.axis_index("beam")
    total_rows = row_dev * lax.axis_size("beam")
    capacity = 2 * total_rows * topk_count // EXPERTS
    score_scale = (entry_width - latent + head_in) ** (-0.5)
    phys_ids = blk_index * pool_dev + jnp.arange(pool_dev, dtype=jnp.int32)
    cache_keys = cache_pool.reshape(group_count, pool_dev * block_len, entry_width)
    cache_values = cache_keys[:, :, :latent]
    recent = jnp.zeros((group_count, beam_count, step_count, entry_width), jnp.bfloat16)
    tables = block_tables
    base_pos = (block_counts * block_len).astype(jnp.float32)
    valid = jnp.arange(max_blocks, dtype=jnp.int32)[None, None, :] < block_counts[:, None, None]
    pair_half = beam_index * unit_dev // FFE
    local_experts = (blk_index * pair_dev + jnp.arange(pair_dev, dtype=jnp.int32)) * 2 + pair_half
    results = []
    for decode_step in range(step_count):
        parent = parents[decode_step]
        recent = jnp.take_along_axis(recent, parent[:, :, None, None], axis=1)
        tables = jnp.take_along_axis(tables, parent[:, :, None], axis=1)
        tokens = embeds[decode_step]
        normed = rms_scale(tokens.astype(jnp.float32), attn_gain).astype(jnp.bfloat16)
        queries = jnp.dot(normed, w_query, preferred_element_type=jnp.float32).astype(jnp.bfloat16)
        queries = queries.reshape(row_dev, heads_dev, w_query.shape[1] // heads_dev)
        position = jnp.repeat(base_pos + decode_step, beam_count)
        query_latent = jnp.einsum(
            "rhn,hnc->rhc", queries[:, :, :head_in], w_key_up, preferred_element_type=jnp.float32
        )
        query_rope = rotate(queries[:, :, head_in:].astype(jnp.float32), position[:, None])
        query_full = jnp.concatenate([query_latent, query_rope], axis=-1).astype(jnp.bfloat16)
        projected = jnp.dot(normed, w_latent, preferred_element_type=jnp.float32)
        new_entry = jnp.concatenate(
            [
                rms_scale(projected[:, :latent], latent_gain),
                rotate(projected[:, latent:], position),
            ],
            axis=-1,
        ).astype(jnp.bfloat16)
        recent = recent.at[:, :, decode_step].set(
            new_entry.reshape(group_count, beam_count, entry_width)
        )
        all_queries = lax.all_gather(query_full, "blk", axis=1, tiled=True)
        head_count = all_queries.shape[1]
        grouped = all_queries.reshape(group_count, beam_count * head_count, entry_width)
        scores = (
            jnp.einsum("gqe,gke->gqk", grouped, cache_keys, preferred_element_type=jnp.float32)
            * score_scale
        )
        block_used = (
            jnp.sum(
                ((tables[:, :, :, None] == phys_ids) & valid[..., None]).astype(jnp.int32), axis=2
            )
            > 0
        )
        key_mask = jnp.repeat(jnp.repeat(block_used, block_len, axis=2), head_count, axis=1)
        top_score, weight_sum, latent_sum = partial_attend(
            scores, key_mask, cache_values, "gqk,gkc->gqc"
        )
        top_score = top_score.reshape(row_dev, head_count)
        weight_sum = weight_sum.reshape(row_dev, head_count)
        latent_sum = latent_sum.reshape(row_dev, head_count, latent)
        merged = combined_all((top_score, weight_sum, latent_sum), "blk", combine)
        head_start = blk_index * heads_dev
        pooled = tuple(
            (lax.dynamic_slice_in_dim(member, head_start, heads_dev, 1) for member in merged)
        )
        recent_rows = recent.reshape(row_dev, step_count, entry_width)[:, : decode_step + 1]
        recent_scores = (
            jnp.einsum("rhe,rse->rhs", query_full, recent_rows, preferred_element_type=jnp.float32)
            * score_scale
        )
        recent_part = partial_attend(
            recent_scores,
            jnp.ones(recent_scores.shape, bool),
            recent_rows[:, :, :latent],
            "rhs,rsc->rhc",
        )
        top_score, weight_sum, latent_sum = combine(pooled, recent_part)
        attended = (latent_sum / weight_sum[..., None]).astype(jnp.bfloat16)
        head_out = jnp.einsum(
            "rhc,hcv->rhv", attended, w_value_up, preferred_element_type=jnp.float32
        ).astype(jnp.bfloat16)
        attn_part = jnp.dot(
            head_out.reshape(row_dev, heads_dev * value_dim),
            w_out,
            preferred_element_type=jnp.float32,
        )
        attn_total = lax.psum(attn_part, "blk")
        resid = tokens.astype(jnp.float32) + attn_total
        ffn_in = rms_scale(resid, ffn_gain).astype(jnp.bfloat16)
        all_rows = lax.all_gather(ffn_in, "beam", axis=0, tiled=True)
        matches = expert_ids[decode_step][:, :, None] == local_experts
        routed = jnp.any(matches, axis=1)
        row_weight = jnp.sum(
            jnp.where(matches, expert_weights[decode_step][:, :, None], 0.0), axis=1
        )
        slot_index = jnp.cumsum(routed.astype(jnp.int32), axis=0) - 1
        slot_index = jnp.where(routed, slot_index, capacity)
        expert_cols = jnp.broadcast_to(
            jnp.arange(pair_dev, dtype=jnp.int32)[None, :], (total_rows, pair_dev)
        )
        row_numbers = jnp.broadcast_to(
            jnp.arange(total_rows, dtype=jnp.int32)[:, None], (total_rows, pair_dev)
        )
        slot_rows = (
            jnp.full((pair_dev, capacity), total_rows, jnp.int32)
            .at[expert_cols, slot_index]
            .set(row_numbers, mode="drop")
        )
        weight_pad = jnp.concatenate([row_weight.T, jnp.zeros((pair_dev, 1), jnp.float32)], axis=1)
        slot_weight = jnp.take_along_axis(weight_pad, slot_rows, axis=1)
        picked = jnp.take(all_rows, slot_rows, axis=0, mode="fill", fill_value=0)
        gate_val = jnp.einsum(
            "ecd,edf->ecf", picked, w_expert_gate, preferred_element_type=jnp.float32
        )
        up_val = jnp.einsum("ecd,edf->ecf", picked, w_expert_up, preferred_element_type=jnp.float32)
        activation = (jax.nn.silu(gate_val) * up_val).astype(jnp.bfloat16)
        down_out = (
            jnp.einsum(
                "ecf,efd->ecd", activation, w_expert_down, preferred_element_type=jnp.float32
            )
            * slot_weight[..., None]
        )
        partial_term = (
            jnp.zeros((total_rows, model_width), jnp.float32)
            .at[slot_rows.reshape(-1)]
            .add(down_out.reshape(-1, model_width), mode="drop")
        )
        shared_act = (
            jax.nn.silu(jnp.dot(ffn_in, w_shared_gate, preferred_element_type=jnp.float32))
            * jnp.dot(ffn_in, w_shared_up, preferred_element_type=jnp.float32)
        ).astype(jnp.bfloat16)
        own_rows = jnp.dot(
            shared_act, w_shared_down, preferred_element_type=jnp.float32
        ) + jnp.where(blk_index == 0, resid, 0.0)
        row_start = beam_index * row_dev
        partial_term = lax.dynamic_update_slice_in_dim(
            partial_term,
            lax.dynamic_slice_in_dim(partial_term, row_start, row_dev, 0) + own_rows,
            row_start,
            0,
        )
        summed = lax.psum_scatter(partial_term, ("blk", "beam"), scatter_dimension=0, tiled=True)
        results.append(summed)
    return jnp.stack(results)


def solution(mesh):
    placed = (
        P(None, "beam", None),
        P(),
        P(None, "blk"),
        P(),
        P(),
        P("blk", None, None),
        P("blk", None, None),
        P("blk", None),
        P(),
        P(None, "blk"),
        P(None, "blk"),
        P("blk", None),
        P("blk", None, "beam"),
        P("blk", None, "beam"),
        P("blk", "beam", None),
        P("beam", "blk", None, None),
        P("beam", None, None),
        P("beam"),
        P(None, "beam", None),
        P(),
        P(),
    )
    return jax.shard_map(
        per_device,
        mesh=mesh,
        in_specs=placed,
        out_specs=P(None, ("blk", "beam"), None),
        check_vma=False,
    )
```

profile of v0, /device:TPU:1, one launch (start us, length us, event | category | flops | bytes accessed | tf_op | source)
XLA Modules:
  0.0 969.4 jit_solution(11336190134766764950)
XLA Ops:
  19.6 20.8 %all_gather.60 = bf16[16,16,576]{2,0,1:T(8,128)(2,1)S(1)} all-gather(bf16[16,1,576]{2,0,1:T(8,128)(2,1)S(1)} %pad_maximum_fusion.4), channel_id=1, replica_groups=mesh['blk'=16,'beam'=8] {'blk'}, dimensions={1}, use_global_device_ids=true | all-gather | bytes 313344 | tf_op jit(solution)/shard_map/all_gather | solution.py:142
  55.1 18.1 %all_gather.65 = bf16[16,16,576]{2,0,1:T(8,128)(2,1)S(1)} all-gather(bf16[16,1,576]{2,0,1:T(8,128)(2,1)S(1)} %pad_maximum_fusion.5), channel_id=1, replica_groups=mesh['blk'=16,'beam'=8] {'blk'}, dimensions={1}, use_global_device_ids=true | all-gather | bytes 313344 | tf_op jit(solution)/shard_map/all_gather | solution.py:142
  77.3 19.4 %all_gather.70 = bf16[16,16,576]{2,0,1:T(8,128)(2,1)S(1)} all-gather(bf16[16,1,576]{2,0,1:T(8,128)(2,1)S(1)} %pad_maximum_fusion.6), channel_id=1, replica_groups=mesh['blk'=16,'beam'=8] {'blk'}, dimensions={1}, use_global_device_ids=true | all-gather | bytes 313344 | tf_op jit(solution)/shard_map/all_gather | solution.py:142
  102.2 19.3 %all_gather.75 = bf16[16,16,576]{2,0,1:T(8,128)(2,1)S(1)} all-gather(bf16[16,1,576]{2,0,1:T(8,128)(2,1)S(1)} %pad_maximum_fusion.7), channel_id=1, replica_groups=mesh['blk'=16,'beam'=8] {'blk'}, dimensions={1}, use_global_device_ids=true | all-gather | bytes 313344 | tf_op jit(solution)/shard_map/all_gather | solution.py:142
  130.3 11.5 %scatter_fusion.3 = s32[2,24]{1,0:T(2,128)S(1)} fusion(s32[2,24]{1,0:T(2,128)S(1)} %broadcast.828.clone, s32[256]{0:T(256)S(1)} %reshape.1849, s32[256]{0:T(256)S(1)} %reshape.1809), kind=kCustom, calls=%fused_computation.22 | custom fusion | bytes 5120 | tf_op jit(solution)/shard_map/scatter | solution.py:208
  158.6 11.5 %scatter_fusion.2 = s32[2,24]{1,0:T(2,128)S(1)} fusion(s32[2,24]{1,0:T(2,128)S(1)} %broadcast.828.clone.1, s32[256]{0:T(256)S(1)} %reshape.1835, s32[256]{0:T(256)S(1)} %reshape.1809), kind=kCustom, calls=%fused_computation.20 | custom fusion | bytes 5120 | tf_op jit(solution)/shard_map/scatter | solution.py:208
  209.0 19.1 %all_gather.61 = f32[16,16,16]{2,1,0:T(8,128)S(1)} all-gather(f32[1,16,16]{2,1,0:T(8,128)S(1)} %all_gather_reshape.36), channel_id=1, replica_groups=mesh['blk'=16,'beam'=8] {'blk'}, dimensions={0}, use_global_device_ids=true | all-gather | bytes 17408 | tf_op jit(solution)/shard_map/all_gather | solution.py:14
  228.2 18.1 %all_gather.62 = f32[16,16,16]{2,1,0:T(8,128)S(1)} all-gather(f32[1,16,16]{2,1,0:T(8,128)S(1)} %all_gather_reshape.37), channel_id=1, replica_groups=mesh['blk'=16,'beam'=8] {'blk'}, dimensions={0}, use_global_device_ids=true | all-gather | bytes 17408 | tf_op jit(solution)/shard_map/all_gather | solution.py:14
  252.9 19.4 %all_gather.66 = f32[16,16,16]{2,1,0:T(8,128)S(1)} all-gather(f32[1,16,16]{2,1,0:T(8,128)S(1)} %all_gather_reshape.39), channel_id=1, replica_groups=mesh['blk'=16,'beam'=8] {'blk'}, dimensions={0}, use_global_device_ids=true | all-gather | bytes 17408 | tf_op jit(solution)/shard_map/all_gather | solution.py:14
  273.0 16.5 %all_gather.67 = f32[16,16,16]{2,1,0:T(8,128)S(1)} all-gather(f32[1,16,16]{2,1,0:T(8,128)S(1)} %all_gather_reshape.40), channel_id=1, replica_groups=mesh['blk'=16,'beam'=8] {'blk'}, dimensions={0}, use_global_device_ids=true | all-gather | bytes 17408 | tf_op jit(solution)/shard_map/all_gather | solution.py:14
  295.8 18.2 %all_gather.71 = f32[16,16,16]{2,1,0:T(8,128)S(1)} all-gather(f32[1,16,16]{2,1,0:T(8,128)S(1)} %all_gather_reshape.42), channel_id=1, replica_groups=mesh['blk'=16,'beam'=8] {'blk'}, dimensions={0}, use_global_device_ids=true | all-gather | bytes 17408 | tf_op jit(solution)/shard_map/all_gather | solution.py:14
  314.8 18.2 %all_gather.72 = f32[16,16,16]{2,1,0:T(8,128)S(1)} all-gather(f32[1,16,16]{2,1,0:T(8,128)S(1)} %all_gather_reshape.43), channel_id=1, replica_groups=mesh['blk'=16,'beam'=8] {'blk'}, dimensions={0}, use_global_device_ids=true | all-gather | bytes 17408 | tf_op jit(solution)/shard_map/all_gather | solution.py:14
  338.0 18.5 %all_gather.76 = f32[16,16,16]{2,1,0:T(8,128)S(1)} all-gather(f32[1,16,16]{2,1,0:T(8,128)} %all_gather_reshape.45), channel_id=1, replica_groups=mesh['blk'=16,'beam'=8] {'blk'}, dimensions={0}, use_global_device_ids=true | all-gather | bytes 17408 | tf_op jit(solution)/shard_map/all_gather | solution.py:14
  357.3 15.7 %all_gather.77 = f32[16,16,16]{2,1,0:T(8,128)S(1)} all-gather(f32[1,16,16]{2,1,0:T(8,128)S(1)} %all_gather_reshape.46), channel_id=1, replica_groups=mesh['blk'=16,'beam'=8] {'blk'}, dimensions={0}, use_global_device_ids=true | all-gather | bytes 17408 | tf_op jit(solution)/shard_map/all_gather | solution.py:14
  390.7 29.7 %while.80 = (s32[]{:T(128)}, f32[16,16]{1,0:T(8,128)S(1)}, f32[16,16]{1,0:T(8,128)S(1)}, f32[16,16,512]{2,1,0:T(8,128)S(1)}, f32[16,16,16]{2,1,0:T(8,128)}, /*in...) while((s32[]{:T(128)}, f32[16,16]{1,0:T(8,128)S(1)}, ...), condition=%wide.region_8.10_spmd, body=%wide.region_7.9_spmd.sunk | while | flops 394757 | bytes 1583255 | solution.py:20
  423.9 29.6 %while.81 = (s32[]{:T(128)}, f32[16,16]{1,0:T(8,128)S(1)}, f32[16,16]{1,0:T(8,128)S(1)}, f32[16,16,512]{2,1,0:T(8,128)S(1)}, f32[16,16,16]{2,1,0:T(8,128)}, /*in...) while((s32[]{:T(128)}, f32[16,16]{1,0:T(8,128)S(1)}, ...), condition=%wide.region_23.28_spmd, body=%wide.region_22.27_spmd.sunk | while | flops 394757 | bytes 1583255 | solution.py:20
  457.2 29.6 %while.82 = (s32[]{:T(128)}, f32[16,16]{1,0:T(8,128)S(1)}, f32[16,16]{1,0:T(8,128)S(1)}, f32[16,16,512]{2,1,0:T(8,128)S(1)}, f32[16,16,16]{2,1,0:T(8,128)}, /*in...) while((s32[]{:T(128)}, f32[16,16]{1,0:T(8,128)S(1)}, ...), condition=%wide.region_40.45_spmd, body=%wide.region_39.44_spmd.sunk | while | flops 394757 | bytes 1583255 | solution.py:20
  490.4 38.8 %while.83 = (s32[]{:T(128)}, f32[16,16]{1,0:T(8,128)S(1)}, f32[16,16]{1,0:T(8,128)}, f32[16,16,512]{2,1,0:T(8,128)S(1)}, f32[16,16,16]{2,1,0:T(8,128)}, /*index=...) while((s32[]{:T(128)}, f32[16,16]{1,0:T(8,128)S(1)}, ...), condition=%wide.region_57.62_spmd, body=%wide.region_56.61_spmd.sunk | while | flops 394757 | bytes 1583255 | solution.py:20
  544.6 134.9 %all-reduce.15.cloned.1.call-done = (f32[16,2048]{1,0:T(8,128)}, f32[16,2048]{1,0:T(8,128)}, f32[16,2048]{1,0:T(8,128)}, f32[16,2048]{1,0:T(8,128)}) async-done(((f32[16,2048]{1,0:T(8,128)}, f32[16,2048]{1,0:T(8,128)}, f32[16,2048]{1,0:T(8,128)}, f32[16,2048]{1,0:T(8,128)}), (f32[16,2048]{1,0:T(8,128)}, f32[16,2048]{1,0:T(8,128)}, f32[16,2048]{1,0:T(8,128)}, ...) | async-done | bytes 524304 | tf_op jit(solution)/shard_map/psum | solution.py:188
  682.2 16.4 %all_gather.79 = bf16[128,2048]{1,0:T(8,128)(2,1)} all-gather(bf16[16,2048]{1,0:T(8,128)(2,1)S(1)} %get-tuple-element.895), channel_id=1, replica_groups=mesh['blk'=16,'beam'=8] {'beam'}, dimensions={0}, use_global_device_ids=true | all-gather | bytes 589824 | tf_op jit(solution)/shard_map/all_gather | solution.py:191
  700.7 14.3 %all_gather.74 = bf16[128,2048]{1,0:T(8,128)(2,1)} all-gather(bf16[16,2048]{1,0:T(8,128)(2,1)S(1)} %get-tuple-element.894), channel_id=1, replica_groups=mesh['blk'=16,'beam'=8] {'beam'}, dimensions={0}, use_global_device_ids=true | all-gather | bytes 589824 | tf_op jit(solution)/shard_map/all_gather | solution.py:191
  715.9 14.3 %all_gather.69 = bf16[128,2048]{1,0:T(8,128)(2,1)} all-gather(bf16[16,2048]{1,0:T(8,128)(2,1)S(1)} %get-tuple-element.893), channel_id=1, replica_groups=mesh['blk'=16,'beam'=8] {'beam'}, dimensions={0}, use_global_device_ids=true | all-gather | bytes 589824 | tf_op jit(solution)/shard_map/all_gather | solution.py:191
  731.1 14.2 %all_gather.64 = bf16[128,2048]{1,0:T(8,128)(2,1)} all-gather(bf16[16,2048]{1,0:T(8,128)(2,1)S(1)} %get-tuple-element.892), channel_id=1, replica_groups=mesh['blk'=16,'beam'=8] {'beam'}, dimensions={0}, use_global_device_ids=true | all-gather | bytes 589824 | tf_op jit(solution)/shard_map/all_gather | solution.py:191
  804.8 153.5 %all-reduce.13.cloned.1.call-done = (f32[128,2048]{1,0:T(8,128)}, f32[128,2048]{1,0:T(8,128)}, f32[128,2048]{1,0:T(8,128)}, f32[128,2048]{1,0:T(8,128)}) async-done(((f32[128,2048]{1,0:T(8,128)}, f32[128,2048]{1,0:T(8,128)}, f32[128,2048]{1,0:T(8,128)}, f32[128,2048]{1,0:T(8,128)}), (f32[128,2048]{1,0:T(8,128)}, f32[128,2048]{1,0:T(8,128)}, f32[128,2048]{1,0:T(8,128)}, ...) | async-done | bytes 4194320
  (624 shorter events, 360.5 us)
Async XLA Ops:
  6.5 744.5 %copy-start = (bf16[2,352,2048]{2,1,0:T(8,128)(2,1)S(1)}, bf16[2,352,2048]{2,1,0:T(8,128)(2,1)}, u32[]{:S(2)}) copy-start(bf16[2,352,2048]{2,1,0:T(8,128)(2,1)} %param.59) | copy-start | bytes 8650756
  6.5 383.1 %all-gather.5.cloned.1.call-start = ((), (), s32[]{:S(2)}) async-start(), calls=%async_computation | async-start | bytes 8912896 | tf_op jit(solution)/shard_map/all_gather | solution.py:14
  49.0 373.9 %all-gather.7.cloned.1.call-start = ((), (), s32[]{:S(2)}) async-start(), calls=%async_computation.1 | async-start | bytes 8912896 | tf_op jit(solution)/shard_map/all_gather | solution.py:14
  76.5 379.6 %all-gather.9.cloned.1.call-start = ((), (), s32[]{:S(2)}) async-start(), calls=%async_computation.2 | async-start | bytes 8912896 | tf_op jit(solution)/shard_map/all_gather | solution.py:14
  101.4 387.8 %all-gather.11.cloned.1.call-start = ((), (), s32[]{:S(2)}) async-start(), calls=%async_computation.3 | async-start | bytes 8912896 | tf_op jit(solution)/shard_map/all_gather | solution.py:14
  126.3 553.2 %all-reduce.15.cloned.1.call-start = ((), (), s32[]{:S(2)}) async-start(), calls=%async_computation.5 | async-start | bytes 1048576 | tf_op jit(solution)/shard_map/psum | solution.py:188
  192.1 58.9 %copy-start.35 = (bf16[16,512]{1,0:T(8,128)(2,1)S(1)}, bf16[16,512]{1,0:T(8,128)(2,1)}, u32[]{:S(2)}) copy-start(bf16[16,512]{1,0:T(8,128)(2,1)} %copy-done.34) | copy-start | bytes 49156
  192.1 58.9 %copy-start.58 = (bf16[16,1,32]{2,0,1:T(8,128)(2,1)S(1)}, bf16[16,1,32]{2,0,1:T(8,128)(2,1)}, u32[]{:S(2)}) copy-start(bf16[16,1,32]{2,0,1:T(8,128)(2,1)} %copy-done.57) | copy-start | bytes 3076
  192.1 58.9 %copy-start.60 = (bf16[16,1,32]{2,0,1:T(8,128)(2,1)S(1)}, bf16[16,1,32]{2,0,1:T(8,128)(2,1)}, u32[]{:S(2)}) copy-start(bf16[16,1,32]{2,0,1:T(8,128)(2,1)} %copy-done.59) | copy-start | bytes 3076
  203.6 90.4 %copy-start.33 = (bf16[16,512]{1,0:T(8,128)(2,1)S(1)}, bf16[16,512]{1,0:T(8,128)(2,1)}, u32[]{:S(2)}) copy-start(bf16[16,512]{1,0:T(8,128)(2,1)} %copy-done.32) | copy-start | bytes 49156
  203.6 90.4 %copy-start.54 = (bf16[16,1,32]{2,0,1:T(8,128)(2,1)S(1)}, bf16[16,1,32]{2,0,1:T(8,128)(2,1)}, u32[]{:S(2)}) copy-start(bf16[16,1,32]{2,0,1:T(8,128)(2,1)} %copy-done.53) | copy-start | bytes 3076
  203.6 90.4 %copy-start.56 = (bf16[16,1,32]{2,0,1:T(8,128)(2,1)S(1)}, bf16[16,1,32]{2,0,1:T(8,128)(2,1)}, u32[]{:S(2)}) copy-start(bf16[16,1,32]{2,0,1:T(8,128)(2,1)} %copy-done.55) | copy-start | bytes 3076
  203.6 132.3 %copy-start.31 = (bf16[16,512]{1,0:T(8,128)(2,1)S(1)}, bf16[16,512]{1,0:T(8,128)(2,1)}, u32[]{:S(2)}) copy-start(bf16[16,512]{1,0:T(8,128)(2,1)} %copy-done.30) | copy-start | bytes 49156
  203.6 132.3 %copy-start.50 = (bf16[16,1,32]{2,0,1:T(8,128)(2,1)S(1)}, bf16[16,1,32]{2,0,1:T(8,128)(2,1)}, u32[]{:S(2)}) copy-start(bf16[16,1,32]{2,0,1:T(8,128)(2,1)} %copy-done.49) | copy-start | bytes 3076
  203.6 132.3 %copy-start.52 = (bf16[16,1,32]{2,0,1:T(8,128)(2,1)S(1)}, bf16[16,1,32]{2,0,1:T(8,128)(2,1)}, u32[]{:S(2)}) copy-start(bf16[16,1,32]{2,0,1:T(8,128)(2,1)} %copy-done.51) | copy-start | bytes 3076
  273.0 111.9 %copy-start.81 = (s32[2,24]{1,0:T(2,128)S(1)}, s32[2,24]{1,0:T(2,128)}, u32[]{:S(2)}) copy-start(s32[2,24]{1,0:T(2,128)} %compare_select_fusion.13) | copy-start | bytes 580
  273.0 113.7 %copy-start.67 = (f32[128,2]{0,1:T(2,128)S(1)}, f32[128,2]{0,1:T(2,128)}, u32[]{:S(2)}) copy-start(f32[128,2]{0,1:T(2,128)} %get-tuple-element.793) | copy-start | bytes 3076
  295.0 94.0 %copy-start.82 = (s32[2,24]{1,0:T(2,128)S(1)}, s32[2,24]{1,0:T(2,128)}, u32[]{:S(2)}) copy-start(s32[2,24]{1,0:T(2,128)} %compare_select_fusion.15) | copy-start | bytes 580
  530.2 149.3 %copy-start.8 = (bf16[4,16,2048]{2,1,0:T(8,128)(2,1)S(1)}, bf16[4,16,2048]{2,1,0:T(8,128)(2,1)}, u32[]{:S(2)}) copy-start(bf16[4,16,2048]{2,1,0:T(8,128)(2,1)} %param.45) | copy-start | bytes 786436
  530.2 150.8 %copy-start.63 = (f32[2048]{0:T(1024)S(1)}, f32[2048]{0:T(1024)}, u32[]{:S(2)}) copy-start(f32[2048]{0:T(1024)} %param.53) | copy-start | bytes 24580
  542.2 416.1 %all-reduce.13.cloned.1.call-start = ((), (), s32[]{:S(2)}) async-start(), calls=%async_computation.4 | async-start | bytes 8388608
  682.2 63.1 %copy-start.15 = (bf16[16,2048]{1,0:T(8,128)(2,1)}, bf16[16,2048]{1,0:T(8,128)(2,1)S(1)}, u32[]{:S(2)}) copy-start(bf16[16,2048]{1,0:T(8,128)(2,1)S(1)} %get-tuple-element.893) | copy-start | bytes 196612
  682.2 63.1 %copy-start.16 = (bf16[16,2048]{1,0:T(8,128)(2,1)}, bf16[16,2048]{1,0:T(8,128)(2,1)S(1)}, u32[]{:S(2)}) copy-start(bf16[16,2048]{1,0:T(8,128)(2,1)S(1)} %get-tuple-element.894) | copy-start | bytes 196612
  682.2 63.1 %copy-start.18 = (bf16[16,2048]{1,0:T(8,128)(2,1)}, bf16[16,2048]{1,0:T(8,128)(2,1)S(1)}, u32[]{:S(2)}) copy-start(bf16[16,2048]{1,0:T(8,128)(2,1)S(1)} %get-tuple-element.895) | copy-start | bytes 196612
  (68 other events, 1006.1 us)
Sparse Core Ops, SparseCore 0:
  49.1 78.4 all-gather.4
  129.8 70.4 all-gather.6
  202.5 71.7 all-gather.8
  276.2 71.4 all-gather.10
  542.4 137.1 all-reduce.14
  804.9 153.3 all-reduce.12
where the time goes:
time: 984 us; the launch traced here: 969 us
  waiting for transfers between devices  288 us (29%)
  blocking collectives  281 us (29%)
  other arithmetic  187 us (19%)
  local copies, waits for them, and re-layouts  113 us (11%)
  matrix products  82.2 us (8%)
  between operations  15.3 us (2%)
    unnamed x7, waiting for transfers between devices  154 us
    all_gather x8, blocking collectives, combined_all(): everything = jax.tree.map(lambda part: lax.all_gather(part, axis), shard)  144 us
    psum x1, waiting for transfers between devices, per_device(): attn_total = lax.psum(attn_part, 'blk')  135 us
    all_gather x4, blocking collectives, per_device(): all_queries = lax.all_gather(query_full, 'blk', axis=1, tiled=True)  77.6 us
    add x60, other arithmetic, combine(): lat_first * scale_first[..., None] + lat_second * scale_second[..., None]  72.7 us
    all_gather x4, blocking collectives, per_device(): all_rows = lax.all_gather(ffn_in, 'beam', axis=0, tiled=True)  59.2 us
    add x60, other arithmetic, combine(): sum_first * scale_first + sum_second * scale_second  53.2 us
    scatter x4, local copies, waits for them, and re-layouts, per_device(): slot_rows = jnp.full((pair_dev, capacity), total_rows, jnp.int32).at[expe...  45.8 us
  transfers between devices with their start and end apart: 6, of which 2 were waited for; matrix products, arithmetic and copies ran while one was open for 24% of the time, Pallas kernels for 0%

commit v1 on v0

--- a/solution.py
+++ b/solution.py
@@ -185,7 +185,7 @@
             w_out,
             preferred_element_type=jnp.float32,
         )
-        attn_total = lax.psum(attn_part, "blk")
+        attn_total = jnp.sum(lax.all_gather(attn_part, "blk"), axis=0)
         resid = tokens.astype(jnp.float32) + attn_total
         ffn_in = rms_scale(resid, ffn_gain).astype(jnp.bfloat16)
         all_rows = lax.all_gather(ffn_in, "beam", axis=0, tiled=True)

time: 984 us -> 943 us (0.958)
  waiting for transfers between devices: 288 us -> 221 us
  other arithmetic: 187 us -> 215 us
    psum x1 -> x0, waiting for transfers between devices: 135 us -> none  [per_device(): attn_total = lax.psum(attn_part, 'blk')]
    all_gather x0 -> x4, waiting for transfers between devices: none -> 67.4 us  [per_device(): attn_total = jnp.sum(lax.all_gather(attn_part, 'blk'), axis=0)]
    add x60, other arithmetic: 53.2 us -> 81.8 us  [combine(): sum_first * scale_first + sum_second * scale_second]
    unnamed x7 -> x10, waiting for transfers between devices: 154 us -> 154 us
  transfers between devices with their start and end apart: 6 -> 9, of which waited for: 2 -> 3; matrix products, arithmetic and copies ran while one was open for 24% -> 34% of each run, Pallas kernels for 0% -> 0%
where the time goes in v1:
time: 943 us; the launch traced here: 928 us
  blocking collectives  282 us (30%)
  waiting for transfers between devices  221 us (23%)
  other arithmetic  215 us (23%)
  local copies, waits for them, and re-layouts  110 us (12%)
  matrix products  82.7 us (9%)
  between operations  14.9 us (2%)
    unnamed x10, waiting for transfers between devices  154 us
    all_gather x8, blocking collectives, combined_all(): everything = jax.tree.map(lambda part: lax.all_gather(part, axis), shard)  146 us
    add x60, other arithmetic, combine(): sum_first * scale_first + sum_second * scale_second  81.8 us
    all_gather x4, blocking collectives, per_device(): all_queries = lax.all_gather(query_full, 'blk', axis=1, tiled=True)  77.2 us
    add x60, other arithmetic, combine(): lat_first * scale_first[..., None] + lat_second * scale_second[..., None]  72.4 us
    all_gather x4, waiting for transfers between devices, per_device(): attn_total = jnp.sum(lax.all_gather(attn_part, 'blk'), axis=0)  67.4 us
    all_gather x4, blocking collectives, per_device(): all_rows = lax.all_gather(ffn_in, 'beam', axis=0, tiled=True)  58.9 us
    scatter x4, local copies, waits for them, and re-layouts, per_device(): slot_rows = jnp.full((pair_dev, capacity), total_rows, jnp.int32).at[expe...  45.8 us
  transfers between devices with their start and end apart: 9, of which 3 were waited for; matrix products, arithmetic and copies ran while one was open for 34% of the time, Pallas kernels for 0%

profile of v1, /device:TPU:1, one launch (start us, length us, event | category | flops | bytes accessed | tf_op | source)
XLA Modules:
  0.0 928.1 jit_solution(6476480056673894762)
XLA Ops:
  19.0 20.8 %all_gather.84 = bf16[16,16,576]{2,0,1:T(8,128)(2,1)S(1)} all-gather(bf16[16,1,576]{2,0,1:T(8,128)(2,1)S(1)} %pad_maximum_fusion.4), channel_id=1, replica_groups=mesh['blk'=16,'beam'=8] {'blk'}, dimensions={1}, use_global_device_ids=true | all-gather | bytes 313344 | tf_op jit(solution)/shard_map/all_gather | solution.py:142
  53.5 18.3 %all_gather.91 = bf16[16,16,576]{2,0,1:T(8,128)(2,1)S(1)} all-gather(bf16[16,1,576]{2,0,1:T(8,128)(2,1)S(1)} %pad_maximum_fusion.5), channel_id=1, replica_groups=mesh['blk'=16,'beam'=8] {'blk'}, dimensions={1}, use_global_device_ids=true | all-gather | bytes 313344 | tf_op jit(solution)/shard_map/all_gather | solution.py:142
  74.8 18.9 %all_gather.98 = bf16[16,16,576]{2,0,1:T(8,128)(2,1)S(1)} all-gather(bf16[16,1,576]{2,0,1:T(8,128)(2,1)S(1)} %pad_maximum_fusion.6), channel_id=1, replica_groups=mesh['blk'=16,'beam'=8] {'blk'}, dimensions={1}, use_global_device_ids=true | all-gather | bytes 313344 | tf_op jit(solution)/shard_map/all_gather | solution.py:142
  98.2 19.3 %all_gather.105 = bf16[16,16,576]{2,0,1:T(8,128)(2,1)S(1)} all-gather(bf16[16,1,576]{2,0,1:T(8,128)(2,1)S(1)} %pad_maximum_fusion.7), channel_id=1, replica_groups=mesh['blk'=16,'beam'=8] {'blk'}, dimensions={1}, use_global_device_ids=true | all-gather | bytes 313344 | tf_op jit(solution)/shard_map/all_gather | solution.py:142
  134.6 11.5 %scatter_fusion.3 = s32[2,24]{1,0:T(2,128)S(1)} fusion(s32[2,24]{1,0:T(2,128)S(1)} %broadcast.828.clone, s32[256]{0:T(256)S(1)} %reshape.1849, s32[256]{0:T(256)S(1)} %reshape.1809), kind=kCustom, calls=%fused_computation.22 | custom fusion | bytes 5120 | tf_op jit(solution)/shard_map/scatter | solution.py:208
  200.9 18.2 %all_gather.85 = f32[16,16,16]{2,1,0:T(8,128)S(1)} all-gather(f32[1,16,16]{2,1,0:T(8,128)S(1)} %all_gather_reshape.36), channel_id=1, replica_groups=mesh['blk'=16,'beam'=8] {'blk'}, dimensions={0}, use_global_device_ids=true | all-gather | bytes 17408 | tf_op jit(solution)/shard_map/all_gather | solution.py:14
  219.1 16.3 %all_gather.86 = f32[16,16,16]{2,1,0:T(8,128)S(1)} all-gather(f32[1,16,16]{2,1,0:T(8,128)S(1)} %all_gather_reshape.37), channel_id=1, replica_groups=mesh['blk'=16,'beam'=8] {'blk'}, dimensions={0}, use_global_device_ids=true | all-gather | bytes 17408 | tf_op jit(solution)/shard_map/all_gather | solution.py:14
  235.4 20.0 %all_gather.92 = f32[16,16,16]{2,1,0:T(8,128)S(1)} all-gather(f32[1,16,16]{2,1,0:T(8,128)S(1)} %all_gather_reshape.39), channel_id=1, replica_groups=mesh['blk'=16,'beam'=8] {'blk'}, dimensions={0}, use_global_device_ids=true | all-gather | bytes 17408 | tf_op jit(solution)/shard_map/all_gather | solution.py:14
  255.4 18.1 %all_gather.93 = f32[16,16,16]{2,1,0:T(8,128)S(1)} all-gather(f32[1,16,16]{2,1,0:T(8,128)S(1)} %all_gather_reshape.40), channel_id=1, replica_groups=mesh['blk'=16,'beam'=8] {'blk'}, dimensions={0}, use_global_device_ids=true | all-gather | bytes 17408 | tf_op jit(solution)/shard_map/all_gather | solution.py:14
  273.4 18.6 %all_gather.99 = f32[16,16,16]{2,1,0:T(8,128)S(1)} all-gather(f32[1,16,16]{2,1,0:T(8,128)S(1)} %all_gather_reshape.42), channel_id=1, replica_groups=mesh['blk'=16,'beam'=8] {'blk'}, dimensions={0}, use_global_device_ids=true | all-gather | bytes 17408 | tf_op jit(solution)/shard_map/all_gather | solution.py:14
  292.0 16.2 %all_gather.100 = f32[16,16,16]{2,1,0:T(8,128)S(1)} all-gather(f32[1,16,16]{2,1,0:T(8,128)S(1)} %all_gather_reshape.43), channel_id=1, replica_groups=mesh['blk'=16,'beam'=8] {'blk'}, dimensions={0}, use_global_device_ids=true | all-gather | bytes 17408 | tf_op jit(solution)/shard_map/all_gather | solution.py:14
  308.2 20.4 %all_gather.106 = f32[16,16,16]{2,1,0:T(8,128)S(1)} all-gather(f32[1,16,16]{2,1,0:T(8,128)S(1)} %all_gather_reshape.45), channel_id=1, replica_groups=mesh['blk'=16,'beam'=8] {'blk'}, dimensions={0}, use_global_device_ids=true | all-gather | bytes 17408 | tf_op jit(solution)/shard_map/all_gather | solution.py:14
  328.6 18.1 %all_gather.107 = f32[16,16,16]{2,1,0:T(8,128)S(1)} all-gather(f32[1,16,16]{2,1,0:T(8,128)S(1)} %all_gather_reshape.46), channel_id=1, replica_groups=mesh['blk'=16,'beam'=8] {'blk'}, dimensions={0}, use_global_device_ids=true | all-gather | bytes 17408 | tf_op jit(solution)/shard_map/all_gather | solution.py:14
  355.8 39.0 %while.80 = (s32[]{:T(128)}, f32[16,16]{1,0:T(8,128)}, f32[16,16]{1,0:T(8,128)}, f32[16,16,512]{2,1,0:T(8,128)S(1)}, f32[16,16,16]{2,1,0:T(8,128)}, /*index=5*/f...) while((s32[]{:T(128)}, f32[16,16]{1,0:T(8,128)}, ...), condition=%wide.region_8.10_spmd, body=%wide.region_7.9_spmd.sunk | while | flops 394757 | bytes 1583255 | solution.py:20
  401.3 39.0 %while.81 = (s32[]{:T(128)}, f32[16,16]{1,0:T(8,128)}, f32[16,16]{1,0:T(8,128)}, f32[16,16,512]{2,1,0:T(8,128)S(1)}, f32[16,16,16]{2,1,0:T(8,128)}, /*index=5*/f...) while((s32[]{:T(128)}, f32[16,16]{1,0:T(8,128)}, ...), condition=%wide.region_23.28_spmd, body=%wide.region_22.27_spmd.sunk | while | flops 394757 | bytes 1583255 | solution.py:20
  446.9 39.0 %while.82 = (s32[]{:T(128)}, f32[16,16]{1,0:T(8,128)}, f32[16,16]{1,0:T(8,128)}, f32[16,16,512]{2,1,0:T(8,128)S(1)}, f32[16,16,16]{2,1,0:T(8,128)}, /*index=5*/f...) while((s32[]{:T(128)}, f32[16,16]{1,0:T(8,128)}, ...), condition=%wide.region_40.45_spmd, body=%wide.region_39.44_spmd.sunk | while | flops 394757 | bytes 1583255 | solution.py:20
  492.5 39.0 %while.83 = (s32[]{:T(128)}, f32[16,16]{1,0:T(8,128)}, f32[16,16]{1,0:T(8,128)}, f32[16,16,512]{2,1,0:T(8,128)S(1)}, f32[16,16,16]{2,1,0:T(8,128)}, /*index=5*/f...) while((s32[]{:T(128)}, f32[16,16]{1,0:T(8,128)}, ...), condition=%wide.region_57.62_spmd, body=%wide.region_56.61_spmd.sunk | while | flops 394757 | bytes 1583255 | solution.py:20
  565.6 22.3 %all-gather.25.cloned.1.call-done = f32[256,2048]{1,0:T(8,128)} async-done(((f32[16,2048]{1,0:T(8,128)}), f32[256,2048]{1,0:T(8,128)}) %all-gather.25.cloned.1.call-update) | async-done | bytes 2097168 | tf_op jit(solution)/shard_map/all_gather | solution.py:188
  589.6 45.0 %all-gather.27.cloned.1.call-done = f32[256,2048]{1,0:T(8,128)} async-done(((f32[16,2048]{1,0:T(8,128)}), f32[256,2048]{1,0:T(8,128)}) %all-gather.27.cloned.1.call-update) | async-done | bytes 2097168 | tf_op jit(solution)/shard_map/all_gather | solution.py:188
  639.3 16.1 %all_gather.111 = bf16[128,2048]{1,0:T(8,128)(2,1)} all-gather(bf16[16,2048]{1,0:T(8,128)(2,1)S(1)} %get-tuple-element.891), channel_id=1, replica_groups=mesh['blk'=16,'beam'=8] {'beam'}, dimensions={0}, use_global_device_ids=true | all-gather | bytes 589824 | tf_op jit(solution)/shard_map/all_gather | solution.py:191
  657.4 14.3 %all_gather.104 = bf16[128,2048]{1,0:T(8,128)(2,1)} all-gather(bf16[16,2048]{1,0:T(8,128)(2,1)S(1)} %get-tuple-element.890), channel_id=1, replica_groups=mesh['blk'=16,'beam'=8] {'beam'}, dimensions={0}, use_global_device_ids=true | all-gather | bytes 589824 | tf_op jit(solution)/shard_map/all_gather | solution.py:191
  672.7 14.2 %all_gather.97 = bf16[128,2048]{1,0:T(8,128)(2,1)} all-gather(bf16[16,2048]{1,0:T(8,128)(2,1)S(1)} %get-tuple-element.889), channel_id=1, replica_groups=mesh['blk'=16,'beam'=8] {'beam'}, dimensions={0}, use_global_device_ids=true | all-gather | bytes 589824 | tf_op jit(solution)/shard_map/all_gather | solution.py:191
  687.7 14.3 %all_gather.90 = bf16[128,2048]{1,0:T(8,128)(2,1)} all-gather(bf16[16,2048]{1,0:T(8,128)(2,1)S(1)} %get-tuple-element.888), channel_id=1, replica_groups=mesh['blk'=16,'beam'=8] {'beam'}, dimensions={0}, use_global_device_ids=true | all-gather | bytes 589824 | tf_op jit(solution)/shard_map/all_gather | solution.py:191
  764.0 153.4 %all-reduce.11.cloned.1.call-done = (f32[128,2048]{1,0:T(8,128)}, f32[128,2048]{1,0:T(8,128)}, f32[128,2048]{1,0:T(8,128)}, f32[128,2048]{1,0:T(8,128)}) async-done(((f32[128,2048]{1,0:T(8,128)}, f32[128,2048]{1,0:T(8,128)}, f32[128,2048]{1,0:T(8,128)}, f32[128,2048]{1,0:T(8,128)}), (f32[128,2048]{1,0:T(8,128)}, f32[128,2048]{1,0:T(8,128)}, f32[128,2048]{1,0:T(8,128)}, ...) | async-done | bytes 4194320
  (587 shorter events, 397.4 us)
Async XLA Ops:
  6.5 702.7 %copy-start = (bf16[2,352,2048]{2,1,0:T(8,128)(2,1)S(1)}, bf16[2,352,2048]{2,1,0:T(8,128)(2,1)}, u32[]{:S(2)}) copy-start(bf16[2,352,2048]{2,1,0:T(8,128)(2,1)} %param.59) | copy-start | bytes 8650756
  6.5 348.1 %all-gather.13.cloned.1.call-start = ((), (), s32[]{:S(2)}) async-start(), calls=%async_computation | async-start | bytes 8912896 | tf_op jit(solution)/shard_map/all_gather | solution.py:14
  48.0 352.3 %all-gather.15.cloned.1.call-start = ((), (), s32[]{:S(2)}) async-start(), calls=%async_computation.1 | async-start | bytes 8912896 | tf_op jit(solution)/shard_map/all_gather | solution.py:14
  74.5 371.3 %all-gather.17.cloned.1.call-start = ((), (), s32[]{:S(2)}) async-start(), calls=%async_computation.2 | async-start | bytes 8912896 | tf_op jit(solution)/shard_map/all_gather | solution.py:14
  97.9 393.5 %all-gather.19.cloned.1.call-start = ((), (), s32[]{:S(2)}) async-start(), calls=%async_computation.3 | async-start | bytes 8912896 | tf_op jit(solution)/shard_map/all_gather | solution.py:14
  121.6 440.4 %all-gather.21.cloned.1.call-start = ((), (), s32[]{:S(2)}) async-start(), calls=%async_computation.4 | async-start | bytes 2228224 | tf_op jit(solution)/shard_map/all_gather | solution.py:188
  219.1 134.8 %copy-start.24 = (f32[16,16,16]{2,1,0:T(8,128)}, f32[16,16,16]{2,1,0:T(8,128)S(1)}, u32[]{:S(2)}) copy-start(f32[16,16,16]{2,1,0:T(8,128)S(1)} %all_gather.85) | copy-start | bytes 49156
  235.4 118.5 %copy-start.25 = (f32[16,16,16]{2,1,0:T(8,128)}, f32[16,16,16]{2,1,0:T(8,128)S(1)}, u32[]{:S(2)}) copy-start(f32[16,16,16]{2,1,0:T(8,128)S(1)} %all_gather.86) | copy-start | bytes 49156
  255.4 98.5 %copy-start.22 = (f32[16,16,16]{2,1,0:T(8,128)}, f32[16,16,16]{2,1,0:T(8,128)S(1)}, u32[]{:S(2)}) copy-start(f32[16,16,16]{2,1,0:T(8,128)S(1)} %all_gather.92) | copy-start | bytes 49156
  273.4 80.4 %copy-start.23 = (f32[16,16,16]{2,1,0:T(8,128)}, f32[16,16,16]{2,1,0:T(8,128)S(1)}, u32[]{:S(2)}) copy-start(f32[16,16,16]{2,1,0:T(8,128)S(1)} %all_gather.93) | copy-start | bytes 49156
  292.0 61.8 %copy-start.20 = (f32[16,16,16]{2,1,0:T(8,128)}, f32[16,16,16]{2,1,0:T(8,128)S(1)}, u32[]{:S(2)}) copy-start(f32[16,16,16]{2,1,0:T(8,128)S(1)} %all_gather.99) | copy-start | bytes 49156
  308.2 45.6 %copy-start.21 = (f32[16,16,16]{2,1,0:T(8,128)}, f32[16,16,16]{2,1,0:T(8,128)S(1)}, u32[]{:S(2)}) copy-start(f32[16,16,16]{2,1,0:T(8,128)S(1)} %all_gather.100) | copy-start | bytes 49156
  355.7 42.3 %copy-start.10 = (bf16[1,512,128]{2,1,0:T(8,128)(2,1)S(1)}, bf16[1,512,128]{2,1,0:T(8,128)(2,1)}, u32[]{:S(2)}) copy-start(bf16[1,512,128]{2,1,0:T(8,128)(2,1)} %param.51) | copy-start | bytes 393220
  400.2 163.6 %all-gather.23.cloned.1.call-start = ((), (), s32[]{:S(2)}) async-start(), calls=%async_computation.5 | async-start | bytes 2228224 | tf_op jit(solution)/shard_map/all_gather | solution.py:188
  445.7 142.2 %all-gather.25.cloned.1.call-start = ((), (), s32[]{:S(2)}) async-start(), calls=%async_computation.6 | async-start | bytes 2228224 | tf_op jit(solution)/shard_map/all_gather | solution.py:188
  491.4 143.3 %all-gather.27.cloned.1.call-start = ((), (), s32[]{:S(2)}) async-start(), calls=%async_computation.7 | async-start | bytes 2228224 | tf_op jit(solution)/shard_map/all_gather | solution.py:188
  536.9 380.4 %all-reduce.11.cloned.1.call-start = ((), (), s32[]{:S(2)}) async-start(), calls=%async_computation.8 | async-start | bytes 8388608
  563.8 73.2 %copy-start.8 = (bf16[4,16,2048]{2,1,0:T(8,128)(2,1)S(1)}, bf16[4,16,2048]{2,1,0:T(8,128)(2,1)}, u32[]{:S(2)}) copy-start(bf16[4,16,2048]{2,1,0:T(8,128)(2,1)} %param.45) | copy-start | bytes 786436
  565.5 72.7 %copy-start.29 = (f32[2048]{0:T(1024)S(1)}, f32[2048]{0:T(1024)}, u32[]{:S(2)}) copy-start(f32[2048]{0:T(1024)} %param.53) | copy-start | bytes 24580
  639.3 47.5 %copy-start.13 = (bf16[16,2048]{1,0:T(8,128)(2,1)}, bf16[16,2048]{1,0:T(8,128)(2,1)S(1)}, u32[]{:S(2)}) copy-start(bf16[16,2048]{1,0:T(8,128)(2,1)S(1)} %get-tuple-element.889) | copy-start | bytes 196612
  639.3 48.4 %copy-start.15 = (bf16[16,2048]{1,0:T(8,128)(2,1)}, bf16[16,2048]{1,0:T(8,128)(2,1)S(1)}, u32[]{:S(2)}) copy-start(bf16[16,2048]{1,0:T(8,128)(2,1)S(1)} %get-tuple-element.890) | copy-start | bytes 196612
  639.3 48.4 %copy-start.16 = (bf16[16,2048]{1,0:T(8,128)(2,1)}, bf16[16,2048]{1,0:T(8,128)(2,1)S(1)}, u32[]{:S(2)}) copy-start(bf16[16,2048]{1,0:T(8,128)(2,1)S(1)} %get-tuple-element.891) | copy-start | bytes 196612
  639.3 62.8 %copy-start.11 = (bf16[16,2048]{1,0:T(8,128)(2,1)}, bf16[16,2048]{1,0:T(8,128)(2,1)S(1)}, u32[]{:S(2)}) copy-start(bf16[16,2048]{1,0:T(8,128)(2,1)S(1)} %get-tuple-element.888) | copy-start | bytes 196612
  657.4 48.3 %copy-start.46 = (pred[2,24]{1,0:T(4,128)(4,1)S(1)}, pred[2,24]{1,0:T(4,128)(4,1)}, u32[]{:S(2)}) copy-start(pred[2,24]{1,0:T(4,128)(4,1)} %compare_and_fusion) | copy-start | bytes 148
  (46 other events, 501.9 us)
Sparse Core Ops, SparseCore 0:
  48.1 78.7 all-gather.12
  129.0 70.3 all-gather.14
  201.6 71.7 all-gather.16
  275.4 71.6 all-gather.18
  400.3 94.1 all-gather.20
  496.5 44.5 all-gather.22
  543.3 44.5 all-gather.24
  590.0 44.5 all-gather.26
  764.1 153.2 all-reduce.10
